TPU v7x, 32 devices: a whole 2x2x4 slice. The times are simulated.
32 devices in a mesh: ctx: 8 (over y, x, core), dp: 4 (over z).
Axes of the slice: x: 2, y: 2, z: 4, core: 2. Of those that a mesh axis runs over, the one named last changes fastest.
Arguments:
- hidden_in: bfloat16 [4, 2048, 2048], P('dp', 'ctx'), may hold values from -6 to 6
- queries: bfloat16 [4, 2048, 2048], P('dp', 'ctx'), may hold values from -1000 to 1000
- norm_gain: bfloat16 [2048], replicated, may hold values from 0.099609375 to 1.8984375
- weight_store: bfloat16 [4, 2048, 512], P('dp', 'ctx'), may hold values from -0.125 to 0.125
- owners: int32 [2], replicated, may hold values from 0 to 3, as said below
- doc_lengths: int32 [4, 4], P('dp'), may hold values from 1 to 1024, 2048 in all within a row
Outputs:
- attended: bfloat16 [4, 2048, 2048], P('dp', 'ctx')
Inputs may be any that keep to these rules, and one draw needn't show every extreme that they name: `owners`: two different data ranks, one of them the last rank 4 - 1; the first owns the key projection, the second the value projection.
All inputs are finite; a program needn't handle non-finite values.
Results may differ from a plain program's by a relative error of at most 0.012.
Values may be sent and summed in bfloat16 or wider, within the bound.
No kernel may reach another device: no remote copies, remote signals or barrier semaphores. Data moves between devices by JAX's collectives and lax.ppermute only.
A program may use at most 64 MiB of HBM per device.

v0:
```python
import jax
import jax.numpy as jnp
from jax import lax
from jax.sharding import PartitionSpec as P

HS = 128
REACH = 4


def from_root(block, axis, owner):
    block = jnp.where(lax.axis_index(axis) == owner, block, jnp.zeros_like(block))
    return lax.psum(block, axis)


def from_behind(x, axis, by):
    size = lax.axis_size(axis)
    pairs = [(i, i + by) for i in range(size) if 0 <= i + by < size]
    return lax.ppermute(x, axis, pairs)


def find_starts(lengths, positions):
    ends = jnp.cumsum(lengths)
    starts = ends - lengths
    below = starts[None, :] <= positions[:, None]
    return jnp.max(jnp.where(below, starts[None, :], 0), axis=1)


def copy_owner(slot_rows, owner):
    return from_root(slot_rows, "dp", owner)


def local(hidden_in, queries, norm_gain, weight_store, owners, doc_lengths):
    tok_rows = hidden_in.shape[1]
    key_width = weight_store.shape[2]
    kv_heads = key_width // HS
    group = queries.shape[2] // key_width
    width_all = (REACH + 1) * tok_rows
    ctx_index = lax.axis_index("ctx")
    xf = hidden_in[0].astype(jnp.float32)
    scaled = (
        xf
        * lax.rsqrt(jnp.mean(xf * xf, axis=-1, keepdims=True) + 1e-05)
        * norm_gain.astype(jnp.float32)
    ).astype(jnp.bfloat16)
    own_slot = weight_store[0]
    key_part = copy_owner(own_slot, owners[0])
    value_part = copy_owner(own_slot, owners[1])
    key_sum = jnp.dot(
        scaled,
        lax.all_gather(key_part, "ctx", axis=0, tiled=True),
        preferred_element_type=jnp.float32,
    )
    value_sum = jnp.dot(
        scaled,
        lax.all_gather(value_part, "ctx", axis=0, tiled=True),
        preferred_element_type=jnp.float32,
    )
    kv_own = jnp.stack([key_sum.astype(jnp.bfloat16), value_sum.astype(jnp.bfloat16)])
    earlier = [from_behind(kv_own, "ctx", back) for back in range(REACH, 0, -1)]
    window = jnp.concatenate(earlier + [kv_own], axis=1)
    q_pos = ctx_index * tok_rows + jnp.arange(tok_rows, dtype=jnp.int32)
    k_pos = (ctx_index - REACH) * tok_rows + jnp.arange(width_all, dtype=jnp.int32)
    q_start = find_starts(doc_lengths[0], q_pos)
    allowed = (k_pos[None, :] >= q_start[:, None]) & (k_pos[None, :] <= q_pos[:, None])
    q_heads = jnp.transpose(queries[0].reshape(tok_rows, kv_heads, group, HS), (1, 2, 0, 3))
    k_heads = jnp.transpose(window[0].reshape(width_all, kv_heads, HS), (1, 0, 2))
    v_heads = jnp.transpose(window[1].reshape(width_all, kv_heads, HS), (1, 0, 2))
    inverse_root = 1.0 / jnp.sqrt(jnp.float32(HS))

    def one_head(args):
        q_one, k_one, v_one = args
        rows = q_one.reshape(group * tok_rows, HS)
        score = jnp.dot(rows, k_one.T, preferred_element_type=jnp.float32)
        score = score.reshape(group, tok_rows, width_all) * inverse_root
        score = jnp.where(allowed[None], score, jnp.float32(-1e30))
        top = jnp.max(score, axis=-1, keepdims=True)
        weight = jnp.exp(score - top)
        total = jnp.sum(weight, axis=-1)
        weight_b = weight.astype(jnp.bfloat16).reshape(group * tok_rows, width_all)
        summed = jnp.dot(weight_b, v_one, preferred_element_type=jnp.float32)
        summed = summed.reshape(group, tok_rows, HS)
        return (summed / total[..., None]).astype(jnp.bfloat16)

    outputs = lax.map(one_head, (q_heads, k_heads, v_heads))
    attended = jnp.transpose(outputs, (2, 0, 1, 3)).reshape(1, tok_rows, kv_heads * group * HS)
    return attended


def solution(mesh):
    return jax.shard_map(
        local,
        mesh=mesh,
        in_specs=(
            P("dp", "ctx", None),
            P("dp", "ctx", None),
            P(),
            P("dp", "ctx", None),
            P(),
            P("dp", None),
        ),
        out_specs=P("dp", "ctx", None),
        check_vma=False,
    )
```

profile of v0, /device:TPU:1, one launch (start us, length us, event | category | flops | bytes accessed | tf_op | source)
XLA Modules:
  0.0 198.7 jit_solution(8778680894563662250)
XLA Ops:
  6.5 1.4 fusion.36
  9.3 1.8 select_bitcast_fusion.1
  11.1 39.7 %all-reduce.3.cloned.1.call-done = (bf16[256,512]{1,0:T(8,128)(2,1)}, bf16[256,512]{1,0:T(8,128)(2,1)}) async-done(((bf16[256,512]{1,0:T(8,128)(2,1)}, bf16[256,512]{1,0:T(8,128)(2,1)}), (bf16[256,512]{1,0:T(8,128)(2,1)}, bf16[256,512]{1,0:T(8,128)(2,1)})) %all-reduce.3.cloned.1.call-update) | async-done | bytes 524304 | tf_op jit(solution)/shard_map/psum | solution.py:12
  53.4 28.6 %all-gather.3.cloned.1.call-done = bf16[2048,512]{1,0:T(8,128)(2,1)} async-done(((bf16[256,512]{1,0:T(8,128)(2,1)}), bf16[2048,512]{1,0:T(8,128)(2,1)}) %all-gather.3.cloned.1.call-update) | async-done | bytes 2097168 | tf_op jit(solution)/shard_map/all_gather | solution.py:50
  82.0 2.3 %fusion.30 = bf16[1,256,512]{2,1,0:T(8,128)(2,1)S(1)} fusion(bf16[2048,512]{1,0:T(8,128)(2,1)} %all-gather.3.cloned.1.call-done, bf16[1,256,2048]{2,1,0:T(8,128)(2,1)S(1)} %copy-done, f32[2048]{0:T(1024)S(1)} %convert_element_type.26, f32[256]{0:T(256)S(1)} %add_rsqrt_fusion), kind=kOutput, calls=%fused_computation.29 | convolution fusion | flops 539099136 | bytes 3417088 | tf_op jit(solution)/shard_map/dot_general | solution.py:48
  84.4 27.5 %all-gather.5.cloned.1.call-done = bf16[2048,512]{1,0:T(8,128)(2,1)} async-done(((bf16[256,512]{1,0:T(8,128)(2,1)}), bf16[2048,512]{1,0:T(8,128)(2,1)}) %all-gather.5.cloned.1.call-update) | async-done | bytes 2097168 | tf_op jit(solution)/shard_map/all_gather | solution.py:55
  111.8 2.3 %fusion.31 = bf16[1,256,512]{2,1,0:T(8,128)(2,1)S(1)} fusion(bf16[2048,512]{1,0:T(8,128)(2,1)} %all-gather.5.cloned.1.call-done, bf16[1,256,2048]{2,1,0:T(8,128)(2,1)S(1)} %copy-done, f32[2048]{0:T(1024)S(1)} %convert_element_type.26, f32[256]{0:T(256)S(1)} %add_rsqrt_fusion), kind=kOutput, calls=%fused_computation.30 | convolution fusion | flops 539099136 | bytes 3417088 | tf_op jit(solution)/shard_map/dot_general | solution.py:53
  115.7 3.8 %collective-permute-start = (bf16[2,256,512]{2,1,0:T(8,128)(2,1)}, bf16[2,256,512]{2,1,0:T(8,128)(2,1)}, u32[]{:S(2)}, u32[]{:S(2)}) collective-permute-start(bf16[2,256,512]{2,1,0:T(8,128)(2,1)} %pad_maximum_fusion), channel_id=1, source_target_pairs={{0,16},{4,20},{8,24},{12,28},{1,17},{5,21},{9,25},{13,29},{2,18},{... | collective-permute-start | bytes 1572872 | tf_op jit(solution)/shard_map/ppermute | solution.py:18
  119.5 2.1 %collective-permute-start.1 = (bf16[2,256,512]{2,1,0:T(8,128)(2,1)}, bf16[2,256,512]{2,1,0:T(8,128)(2,1)}, u32[]{:S(2)}, u32[]{:S(2)}) collective-permute-start(bf16[2,256,512]{2,1,0:T(8,128)(2,1)} %pad_maximum_fusion), channel_id=1, source_target_pairs={{0,12},{4,16},{8,20},{12,24},{16,28},{1,13},{5,17},{9,21},{13,25},... | collective-permute-start | bytes 1572872 | tf_op jit(solution)/shard_map/ppermute | solution.py:18
  121.6 2.9 %collective-permute-start.2 = (bf16[2,256,512]{2,1,0:T(8,128)(2,1)}, bf16[2,256,512]{2,1,0:T(8,128)(2,1)}, u32[]{:S(2)}, u32[]{:S(2)}) collective-permute-start(bf16[2,256,512]{2,1,0:T(8,128)(2,1)} %pad_maximum_fusion), channel_id=1, source_target_pairs={{0,8},{4,12},{8,16},{12,20},{16,24},{20,28},{1,9},{5,13},{9,17},{1... | collective-permute-start | bytes 1572872 | tf_op jit(solution)/shard_map/ppermute | solution.py:18
  124.5 1.9 collective-permute-start.3
  127.1 25.4 %collective-permute-done = bf16[2,256,512]{2,1,0:T(8,128)(2,1)} collective-permute-done((bf16[2,256,512]{2,1,0:T(8,128)(2,1)}, bf16[2,256,512]{2,1,0:T(8,128)(2,1)}, u32[]{:S(2)}, u32[]{:S(2)}) %collective-permute-start) | collective-permute-done | bytes 524320 | tf_op jit(solution)/shard_map/ppermute | solution.py:18
  152.5 1.1 constant_dynamic-update-slice_fusion.4
  153.6 5.2 %collective-permute-done.1 = bf16[2,256,512]{2,1,0:T(8,128)(2,1)} collective-permute-done((bf16[2,256,512]{2,1,0:T(8,128)(2,1)}, bf16[2,256,512]{2,1,0:T(8,128)(2,1)}, u32[]{:S(2)}, u32[]{:S(2)}) %collective-permute-start.1) | collective-permute-done | bytes 524320 | tf_op jit(solution)/shard_map/ppermute | solution.py:18
  158.8 1.1 constant_dynamic-update-slice_fusion.3
  159.9 1.1 constant_dynamic-update-slice_fusion.2
  161.0 1.1 constant_dynamic-update-slice_fusion.1
  162.1 1.2 fusion.35
  163.4 3.6 %reshape_squeeze.10 = bf16[1280,4,128]{2,1,0:T(4,128)(2,1)} reshape(bf16[1,1280,512]{2,1,0:T(8,128)(2,1)} %get-tuple-element.96) | data formatting | bytes 2621440 | tf_op jit(solution)/shard_map/reshape;squeeze | solution.py:66
  166.9 1.2 reshape_squeeze.11
  168.2 3.1 %copy_bitcast_fusion = (bf16[4,1280,128]{2,1,0:T(8,128)(2,1)}, bf16[4,1280,128]{2,1,0:T(8,128)(2,1)S(1)}) fusion(bf16[1280,4,128]{2,1,0:T(4,128)(2,1)} %reshape_squeeze.11, bf16[1280,4,128]{2,1,0:T(4,128)(2,1)} %reshape_squeeze.10), kind=kLoop, calls=%fused_computation.25 | loop fusion | bytes 5242880 | tf_op jit(solution)/shard_map/transpose | solution.py:67
  171.3 18.5 %while.11 = (s32[]{:T(128)}, bf16[4,4,256,128]{3,2,1,0:T(8,128)(2,1)S(1)}, bf16[4,4,256,128]{2,3,1,0:T(8,128)(2,1)S(1)}, bf16[4,1280,128]{2,1,0:T(8,128)(2,1)S(1...) while((s32[]{:T(128)}, ...), condition=%wide.region_8.9_spmd.clone, body=%wide.region_5.8_spmd.clone.sunk | while | flops 681506816 | bytes 17593436 | solution.py:84
  171.6 1.3 fusion.46
  172.9 1.0 fusion.47
  173.9 2.0 %fusion.48 = bf16[4,4,256,128]{3,2,1,0:T(8,128)(2,1)S(1)} fusion(bf16[4,4,256,128]{3,2,1,0:T(8,128)(2,1)S(1)} %get-tuple-element.166, s32[]{:T(128)} %get-tuple-element.165, f32[4,256,1280]{2,1,0:T(8,128)S(1)} %get-tuple-element.154, f32[4,256]{1,0:T(4,128)S(1)} %get-tuple-element.155, bf16[4,1280,128]{2,1,0:T(8,128)(2,1)} %get-tuple-element.178, ...), kind=kOutput, calls=%fused_computation.11.clone.1 | convolution fusion | flops 338427904 | bytes 5841920 | tf_op jit(solution)/shard_map/while/body/eval_jaxpr/dot_general | solution.py:80
  176.2 1.3 fusion.46
  178.5 2.0 %fusion.48 = bf16[4,4,256,128]{3,2,1,0:T(8,128)(2,1)S(1)} fusion(bf16[4,4,256,128]{3,2,1,0:T(8,128)(2,1)S(1)} %get-tuple-element.166, s32[]{:T(128)} %get-tuple-element.165, f32[4,256,1280]{2,1,0:T(8,128)S(1)} %get-tuple-element.154, f32[4,256]{1,0:T(4,128)S(1)} %get-tuple-element.155, bf16[4,1280,128]{2,1,0:T(8,128)(2,1)} %get-tuple-element.178, ...), kind=kOutput, calls=%fused_computation.11.clone.1 | convolution fusion | flops 338427904 | bytes 5841920 | tf_op jit(solution)/shard_map/while/body/eval_jaxpr/dot_general | solution.py:80
  180.8 1.3 fusion.46
  183.1 2.0 %fusion.48 = bf16[4,4,256,128]{3,2,1,0:T(8,128)(2,1)S(1)} fusion(bf16[4,4,256,128]{3,2,1,0:T(8,128)(2,1)S(1)} %get-tuple-element.166, s32[]{:T(128)} %get-tuple-element.165, f32[4,256,1280]{2,1,0:T(8,128)S(1)} %get-tuple-element.154, f32[4,256]{1,0:T(4,128)S(1)} %get-tuple-element.155, bf16[4,1280,128]{2,1,0:T(8,128)(2,1)} %get-tuple-element.178, ...), kind=kOutput, calls=%fused_computation.11.clone.1 | convolution fusion | flops 338427904 | bytes 5841920 | tf_op jit(solution)/shard_map/while/body/eval_jaxpr/dot_general | solution.py:80
  185.5 1.3 fusion.46
  187.7 2.0 %fusion.48 = bf16[4,4,256,128]{3,2,1,0:T(8,128)(2,1)S(1)} fusion(bf16[4,4,256,128]{3,2,1,0:T(8,128)(2,1)S(1)} %get-tuple-element.166, s32[]{:T(128)} %get-tuple-element.165, f32[4,256,1280]{2,1,0:T(8,128)S(1)} %get-tuple-element.154, f32[4,256]{1,0:T(4,128)S(1)} %get-tuple-element.155, bf16[4,1280,128]{2,1,0:T(8,128)(2,1)} %get-tuple-element.178, ...), kind=kOutput, calls=%fused_computation.11.clone.1 | convolution fusion | flops 338427904 | bytes 5841920 | tf_op jit(solution)/shard_map/while/body/eval_jaxpr/dot_general | solution.py:80
  190.6 1.6 reshape.47
  (38 shorter events, 9.8 us)
Async XLA Ops:
  6.5 46.5 %copy-start = (bf16[1,256,2048]{2,1,0:T(8,128)(2,1)S(1)}, bf16[1,256,2048]{2,1,0:T(8,128)(2,1)}, u32[]{:S(2)}) copy-start(bf16[1,256,2048]{2,1,0:T(8,128)(2,1)} %param.8) | copy-start | bytes 3145732
  6.5 44.3 %all-reduce.3.cloned.1.call-start = ((), (), s32[]{:S(2)}) async-start(), calls=%async_computation.2 | async-start | bytes 1048576 | tf_op jit(solution)/shard_map/psum | solution.py:12
  11.1 70.9 %all-gather.3.cloned.1.call-start = ((), (), s32[]{:S(2)}) async-start(), calls=%async_computation | async-start | bytes 2359296 | tf_op jit(solution)/shard_map/all_gather | solution.py:50
  50.8 61.0 %all-gather.5.cloned.1.call-start = ((), (), s32[]{:S(2)}) async-start(), calls=%async_computation.1 | async-start | bytes 2359296 | tf_op jit(solution)/shard_map/all_gather | solution.py:55
  84.3 37.3 %copy-start.4 = (s32[1,4]{1,0:T(1,128)S(1)}, s32[1,4]{1,0:T(1,128)}, u32[]{:S(2)}) copy-start(s32[1,4]{1,0:T(1,128)} %param.13) | copy-start | bytes 52
  84.3 42.1 %copy-start.1 = (bf16[1,256,2048]{2,1,0:T(8,128)(2,1)S(1)}, bf16[1,256,2048]{2,1,0:T(8,128)(2,1)}, u32[]{:S(2)}) copy-start(bf16[1,256,2048]{2,1,0:T(8,128)(2,1)} %param.9) | copy-start | bytes 3145732
  114.2 0.7 copy-start.2
  115.7 36.8 %collective-permute-start = (bf16[2,256,512]{2,1,0:T(8,128)(2,1)}, bf16[2,256,512]{2,1,0:T(8,128)(2,1)}, u32[]{:S(2)}, u32[]{:S(2)}) collective-permute-start(bf16[2,256,512]{2,1,0:T(8,128)(2,1)} %pad_maximum_fusion), channel_id=1, source_target_pairs={{0,16},{4,20},{8,24},{12,28},{1,17},{5,21},{9,25},{13,29},{2,18},{... | collective-permute-start | bytes 1572872 | tf_op jit(solution)/shard_map/ppermute | solution.py:18
  119.5 39.3 %collective-permute-start.1 = (bf16[2,256,512]{2,1,0:T(8,128)(2,1)}, bf16[2,256,512]{2,1,0:T(8,128)(2,1)}, u32[]{:S(2)}, u32[]{:S(2)}) collective-permute-start(bf16[2,256,512]{2,1,0:T(8,128)(2,1)} %pad_maximum_fusion), channel_id=1, source_target_pairs={{0,12},{4,16},{8,20},{12,24},{16,28},{1,13},{5,17},{9,21},{13,25},... | collective-permute-start | bytes 1572872 | tf_op jit(solution)/shard_map/ppermute | solution.py:18
  121.6 38.3 %collective-permute-start.2 = (bf16[2,256,512]{2,1,0:T(8,128)(2,1)}, bf16[2,256,512]{2,1,0:T(8,128)(2,1)}, u32[]{:S(2)}, u32[]{:S(2)}) collective-permute-start(bf16[2,256,512]{2,1,0:T(8,128)(2,1)} %pad_maximum_fusion), channel_id=1, source_target_pairs={{0,8},{4,12},{8,16},{12,20},{16,24},{20,28},{1,9},{5,13},{9,17},{1... | collective-permute-start | bytes 1572872 | tf_op jit(solution)/shard_map/ppermute | solution.py:18
  124.5 36.5 %collective-permute-start.3 = (bf16[2,256,512]{2,1,0:T(8,128)(2,1)}, bf16[2,256,512]{2,1,0:T(8,128)(2,1)}, u32[]{:S(2)}, u32[]{:S(2)}) collective-permute-start(bf16[2,256,512]{2,1,0:T(8,128)(2,1)} %pad_maximum_fusion), channel_id=1, source_target_pairs={{0,4},{4,8},{8,12},{12,16},{16,20},{20,24},{24,28},{1,5},{5,9},{9,... | collective-permute-start | bytes 1572872 | tf_op jit(solution)/shard_map/ppermute | solution.py:18
  127.1 35.0 %copy-start.3 = (bf16[1,256,512]{2,1,0:T(8,128)(2,1)S(1)}, bf16[1,256,512]{2,1,0:T(8,128)(2,1)}, u32[]{:S(2)}) copy-start(bf16[1,256,512]{2,1,0:T(8,128)(2,1)} %copy-done.2) | copy-start | bytes 786436
Sparse Core Ops, SparseCore 0:
  11.2 39.5 all-reduce.2
  52.7 29.2 all-gather.2
  83.9 27.8 all-gather.4
where the time goes:
time: 199 us
  waiting for transfers between devices  127 us (64%)
  local copies, waits for them, and re-layouts  18.5 us (9%)
  matrix products  17.9 us (9%)
  between operations  14.6 us (7%)
  starting transfers between devices  10.8 us (5%)
  other arithmetic  9.72 us (5%)
    psum x1, waiting for transfers between devices, from_root(): return lax.psum(block, axis)  39.7 us
    ppermute x4, waiting for transfers between devices, from_behind(): return lax.ppermute(x, axis, pairs)  30.6 us
    all_gather x1, waiting for transfers between devices, local(): lax.all_gather(key_part, 'ctx', axis=0, tiled=True)  28.6 us
    all_gather x1, waiting for transfers between devices, local(): lax.all_gather(value_part, 'ctx', axis=0, tiled=True)  27.5 us
    ppermute x4, starting transfers between devices, from_behind(): return lax.ppermute(x, axis, pairs)  10.7 us
    dot_general x4, matrix products, one_head(): summed = jnp.dot(weight_b, v_one, preferred_element_type=jnp.float32)  8.07 us
    unnamed x15, local copies, waits for them, and re-layouts  5.55 us
    dot_general x4, matrix products, one_head(): score = jnp.dot(rows, k_one.T, preferred_element_type=jnp.float32)  5.14 us
  transfers between devices with their start and end apart: 7, of which 5 were waited for; matrix products, arithmetic and copies ran while one was open for 4% of the time, Pallas kernels for 0%

commit v1 on v0

--- a/solution.py
+++ b/solution.py
@@ -9,7 +9,7 @@
 
 def from_root(block, axis, owner):
     block = jnp.where(lax.axis_index(axis) == owner, block, jnp.zeros_like(block))
-    return lax.psum(block, axis)
+    return jnp.sum(lax.all_gather(block, axis), axis=0)
 
 
 def from_behind(x, axis, by):

time: 199 us -> 217 us (1.090)
  waiting for transfers between devices: 127 us -> 142 us
  other arithmetic: 9.72 us -> 12.8 us
    all_gather x0 -> x2, waiting for transfers between devices: none -> 56 us  [from_root(): return jnp.sum(lax.all_gather(block, axis), axis=0)]
    psum x1 -> x0, waiting for transfers between devices: 39.7 us -> none  [from_root(): return lax.psum(block, axis)]
    reduce_sum x0 -> x2, other arithmetic: none -> 4.31 us  [from_root(): return jnp.sum(lax.all_gather(block, axis), axis=0)]
    unnamed x15 -> x17, local copies, waits for them, and re-layouts: 5.55 us -> 5.55 us
  transfers between devices with their start and end apart: 7 -> 8, of which waited for: 5 -> 6; matrix products, arithmetic and copies ran while one was open for 4% -> 5% of each run, Pallas kernels for 0% -> 0%
where the time goes in v1:
time: 217 us; the launch traced here: 216 us
  waiting for transfers between devices  142 us (65%)
  local copies, waits for them, and re-layouts  18.4 us (8%)
  matrix products  17.9 us (8%)
  between operations  14.5 us (7%)
  other arithmetic  12.8 us (6%)
  starting transfers between devices  10.9 us (5%)
    all_gather x2, waiting for transfers between devices, from_root(): return jnp.sum(lax.all_gather(block, axis), axis=0)  56 us
    ppermute x4, waiting for transfers between devices, from_behind(): return lax.ppermute(x, axis, pairs)  30.6 us
    all_gather x1, waiting for transfers between devices, local(): lax.all_gather(value_part, 'ctx', axis=0, tiled=True)  27.3 us
    all_gather x1, waiting for transfers between devices, local(): lax.all_gather(key_part, 'ctx', axis=0, tiled=True)  27.2 us
    ppermute x4, starting transfers between devices, from_behind(): return lax.ppermute(x, axis, pairs)  10.7 us
    dot_general x4, matrix products, one_head(): summed = jnp.dot(weight_b, v_one, preferred_element_type=jnp.float32)  8.07 us
    unnamed x17, local copies, waits for them, and re-layouts  5.55 us
    dot_general x4, matrix products, one_head(): score = jnp.dot(rows, k_one.T, preferred_element_type=jnp.float32)  5.14 us
  transfers between devices with their start and end apart: 8, of which 6 were waited for; matrix products, arithmetic and copies ran while one was open for 5% of the time, Pallas kernels for 0%

profile of v1, /device:TPU:1, one launch (start us, length us, event | category | flops | bytes accessed | tf_op | source)
XLA Modules:
  0.0 216.5 jit_solution(1968186750473574653)
XLA Ops:
  6.5 1.3 fusion.36
  9.1 1.9 broadcast_select_fusion.1
  11.8 29.2 %all-gather.5.cloned.1.call-done = bf16[4,256,512]{2,1,0:T(8,128)(2,1)} async-done(((bf16[1,256,512]{2,1,0:T(8,128)(2,1)}), bf16[4,256,512]{2,1,0:T(8,128)(2,1)}) %all-gather.5.cloned.1.call-update) | async-done | bytes 1048592 | tf_op jit(solution)/shard_map/all_gather | solution.py:12
  41.0 2.2 reduce_sum.43
  43.2 26.8 %all-gather.9.cloned.1.call-done = bf16[4,256,512]{2,1,0:T(8,128)(2,1)} async-done(((bf16[1,256,512]{2,1,0:T(8,128)(2,1)}), bf16[4,256,512]{2,1,0:T(8,128)(2,1)}) %all-gather.9.cloned.1.call-update) | async-done | bytes 1048592 | tf_op jit(solution)/shard_map/all_gather | solution.py:12
  70.0 2.2 reduce_sum.44
  72.7 27.2 %all-gather.7.cloned.1.call-done = bf16[2048,512]{1,0:T(8,128)(2,1)} async-done(((bf16[256,512]{1,0:T(8,128)(2,1)}), bf16[2048,512]{1,0:T(8,128)(2,1)}) %all-gather.7.cloned.1.call-update) | async-done | bytes 2097168 | tf_op jit(solution)/shard_map/all_gather | solution.py:50
  99.9 2.3 %fusion.30 = bf16[1,256,512]{2,1,0:T(8,128)(2,1)S(1)} fusion(bf16[2048,512]{1,0:T(8,128)(2,1)} %all-gather.7.cloned.1.call-done, bf16[1,256,2048]{2,1,0:T(8,128)(2,1)S(1)} %copy-done, f32[2048]{0:T(1024)S(1)} %convert_element_type.30, f32[256]{0:T(256)S(1)} %add_rsqrt_fusion), kind=kOutput, calls=%fused_computation.29 | convolution fusion | flops 539099136 | bytes 3417088 | tf_op jit(solution)/shard_map/dot_general | solution.py:48
  102.3 27.3 %all-gather.11.cloned.1.call-done = bf16[2048,512]{1,0:T(8,128)(2,1)} async-done(((bf16[256,512]{1,0:T(8,128)(2,1)}), bf16[2048,512]{1,0:T(8,128)(2,1)}) %all-gather.11.cloned.1.call-update) | async-done | bytes 2097168 | tf_op jit(solution)/shard_map/all_gather | solution.py:55
  129.6 2.3 %fusion.31 = bf16[1,256,512]{2,1,0:T(8,128)(2,1)S(1)} fusion(bf16[2048,512]{1,0:T(8,128)(2,1)} %all-gather.11.cloned.1.call-done, bf16[1,256,2048]{2,1,0:T(8,128)(2,1)S(1)} %copy-done, f32[2048]{0:T(1024)S(1)} %convert_element_type.30, f32[256]{0:T(256)S(1)} %add_rsqrt_fusion), kind=kOutput, calls=%fused_computation.30 | convolution fusion | flops 539099136 | bytes 3417088 | tf_op jit(solution)/shard_map/dot_general | solution.py:53
  133.5 3.8 %collective-permute-start = (bf16[2,256,512]{2,1,0:T(8,128)(2,1)}, bf16[2,256,512]{2,1,0:T(8,128)(2,1)}, u32[]{:S(2)}, u32[]{:S(2)}) collective-permute-start(bf16[2,256,512]{2,1,0:T(8,128)(2,1)} %pad_maximum_fusion), channel_id=1, source_target_pairs={{0,16},{4,20},{8,24},{12,28},{1,17},{5,21},{9,25},{13,29},{2,18},{... | collective-permute-start | bytes 1572872 | tf_op jit(solution)/shard_map/ppermute | solution.py:18
  137.3 2.1 collective-permute-start.1
  139.3 3.0 %collective-permute-start.2 = (bf16[2,256,512]{2,1,0:T(8,128)(2,1)}, bf16[2,256,512]{2,1,0:T(8,128)(2,1)}, u32[]{:S(2)}, u32[]{:S(2)}) collective-permute-start(bf16[2,256,512]{2,1,0:T(8,128)(2,1)} %pad_maximum_fusion), channel_id=1, source_target_pairs={{0,8},{4,12},{8,16},{12,20},{16,24},{20,28},{1,9},{5,13},{9,17},{1... | collective-permute-start | bytes 1572872 | tf_op jit(solution)/shard_map/ppermute | solution.py:18
  142.3 1.9 collective-permute-start.3
  144.9 25.4 %collective-permute-done = bf16[2,256,512]{2,1,0:T(8,128)(2,1)} collective-permute-done((bf16[2,256,512]{2,1,0:T(8,128)(2,1)}, bf16[2,256,512]{2,1,0:T(8,128)(2,1)}, u32[]{:S(2)}, u32[]{:S(2)}) %collective-permute-start) | collective-permute-done | bytes 524320 | tf_op jit(solution)/shard_map/ppermute | solution.py:18
  171.3 5.3 %collective-permute-done.1 = bf16[2,256,512]{2,1,0:T(8,128)(2,1)} collective-permute-done((bf16[2,256,512]{2,1,0:T(8,128)(2,1)}, bf16[2,256,512]{2,1,0:T(8,128)(2,1)}, u32[]{:S(2)}, u32[]{:S(2)}) %collective-permute-start.1) | collective-permute-done | bytes 524320 | tf_op jit(solution)/shard_map/ppermute | solution.py:18
  177.7 1.1 constant_dynamic-update-slice_fusion.2
  178.8 1.1 constant_dynamic-update-slice_fusion.1
  179.9 1.2 fusion.35
  181.2 3.6 %reshape_squeeze.10 = bf16[1280,4,128]{2,1,0:T(4,128)(2,1)} reshape(bf16[1,1280,512]{2,1,0:T(8,128)(2,1)} %get-tuple-element.102) | data formatting | bytes 2621440 | tf_op jit(solution)/shard_map/reshape;squeeze | solution.py:66
  184.7 1.2 reshape_squeeze.11
  185.9 3.1 %copy_bitcast_fusion = (bf16[4,1280,128]{2,1,0:T(8,128)(2,1)}, bf16[4,1280,128]{2,1,0:T(8,128)(2,1)S(1)}) fusion(bf16[1280,4,128]{2,1,0:T(4,128)(2,1)} %reshape_squeeze.11, bf16[1280,4,128]{2,1,0:T(4,128)(2,1)} %reshape_squeeze.10), kind=kLoop, calls=%fused_computation.25 | loop fusion | bytes 5242880 | tf_op jit(solution)/shard_map/transpose | solution.py:67
  189.1 18.5 %while.11 = (s32[]{:T(128)}, bf16[4,4,256,128]{3,2,1,0:T(8,128)(2,1)S(1)}, bf16[4,4,256,128]{2,3,1,0:T(8,128)(2,1)S(1)}, bf16[4,1280,128]{2,1,0:T(8,128)(2,1)S(1...) while((s32[]{:T(128)}, ...), condition=%wide.region_8.9_spmd.clone, body=%wide.region_5.8_spmd.clone.sunk | while | flops 681506816 | bytes 17593436 | solution.py:84
  189.4 1.3 fusion.46
  191.6 2.0 fusion.48
  194.0 1.3 fusion.46
  196.3 2.0 fusion.48
  198.6 1.3 fusion.46
  200.9 2.0 fusion.48
  203.2 1.3 fusion.46
  205.5 2.0 fusion.48
  208.3 1.6 reshape.41
  (45 shorter events, 11.7 us)
Async XLA Ops:
  6.5 34.5 %all-gather.5.cloned.1.call-start = ((), (), s32[]{:S(2)}) async-start(), calls=%async_computation | async-start | bytes 1310720 | tf_op jit(solution)/shard_map/all_gather | solution.py:12
  9.1 63.2 %copy-start.4 = (bf16[2048]{0:T(1024)(128)(2,1)S(1)}, bf16[2048]{0:T(1024)(128)(2,1)}, u32[]{:S(2)}) copy-start(bf16[2048]{0:T(1024)(128)(2,1)} %param.10) | copy-start | bytes 12292
  9.1 63.2 %copy-start.5 = (s32[1,4]{1,0:T(1,128)S(1)}, s32[1,4]{1,0:T(1,128)}, u32[]{:S(2)}) copy-start(s32[1,4]{1,0:T(1,128)} %param.13) | copy-start | bytes 52
  9.1 63.3 %copy-start = (bf16[1,256,2048]{2,1,0:T(8,128)(2,1)S(1)}, bf16[1,256,2048]{2,1,0:T(8,128)(2,1)}, u32[]{:S(2)}) copy-start(bf16[1,256,2048]{2,1,0:T(8,128)(2,1)} %param.8) | copy-start | bytes 3145732
  11.0 59.1 %all-gather.9.cloned.1.call-start = ((), (), s32[]{:S(2)}) async-start(), calls=%async_computation.2 | async-start | bytes 1310720 | tf_op jit(solution)/shard_map/all_gather | solution.py:12
  11.7 88.2 %all-gather.7.cloned.1.call-start = ((), (), s32[]{:S(2)}) async-start(), calls=%async_computation.1 | async-start | bytes 2359296 | tf_op jit(solution)/shard_map/all_gather | solution.py:50
  43.2 86.4 %all-gather.11.cloned.1.call-start = ((), (), s32[]{:S(2)}) async-start(), calls=%async_computation.3 | async-start | bytes 2359296 | tf_op jit(solution)/shard_map/all_gather | solution.py:55
  102.3 42.0 %copy-start.1 = (bf16[1,256,2048]{2,1,0:T(8,128)(2,1)S(1)}, bf16[1,256,2048]{2,1,0:T(8,128)(2,1)}, u32[]{:S(2)}) copy-start(bf16[1,256,2048]{2,1,0:T(8,128)(2,1)} %param.9) | copy-start | bytes 3145732
  131.9 0.7 copy-start.2
  133.5 36.8 %collective-permute-start = (bf16[2,256,512]{2,1,0:T(8,128)(2,1)}, bf16[2,256,512]{2,1,0:T(8,128)(2,1)}, u32[]{:S(2)}, u32[]{:S(2)}) collective-permute-start(bf16[2,256,512]{2,1,0:T(8,128)(2,1)} %pad_maximum_fusion), channel_id=1, source_target_pairs={{0,16},{4,20},{8,24},{12,28},{1,17},{5,21},{9,25},{13,29},{2,18},{... | collective-permute-start | bytes 1572872 | tf_op jit(solution)/shard_map/ppermute | solution.py:18
  137.3 39.3 %collective-permute-start.1 = (bf16[2,256,512]{2,1,0:T(8,128)(2,1)}, bf16[2,256,512]{2,1,0:T(8,128)(2,1)}, u32[]{:S(2)}, u32[]{:S(2)}) collective-permute-start(bf16[2,256,512]{2,1,0:T(8,128)(2,1)} %pad_maximum_fusion), channel_id=1, source_target_pairs={{0,12},{4,16},{8,20},{12,24},{16,28},{1,13},{5,17},{9,21},{13,25},... | collective-permute-start | bytes 1572872 | tf_op jit(solution)/shard_map/ppermute | solution.py:18
  139.3 38.3 %collective-permute-start.2 = (bf16[2,256,512]{2,1,0:T(8,128)(2,1)}, bf16[2,256,512]{2,1,0:T(8,128)(2,1)}, u32[]{:S(2)}, u32[]{:S(2)}) collective-permute-start(bf16[2,256,512]{2,1,0:T(8,128)(2,1)} %pad_maximum_fusion), channel_id=1, source_target_pairs={{0,8},{4,12},{8,16},{12,20},{16,24},{20,28},{1,9},{5,13},{9,17},{1... | collective-permute-start | bytes 1572872 | tf_op jit(solution)/shard_map/ppermute | solution.py:18
  142.3 36.5 %collective-permute-start.3 = (bf16[2,256,512]{2,1,0:T(8,128)(2,1)}, bf16[2,256,512]{2,1,0:T(8,128)(2,1)}, u32[]{:S(2)}, u32[]{:S(2)}) collective-permute-start(bf16[2,256,512]{2,1,0:T(8,128)(2,1)} %pad_maximum_fusion), channel_id=1, source_target_pairs={{0,4},{4,8},{8,12},{12,16},{16,20},{20,24},{24,28},{1,5},{5,9},{9,... | collective-permute-start | bytes 1572872 | tf_op jit(solution)/shard_map/ppermute | solution.py:18
  144.9 35.0 %copy-start.3 = (bf16[1,256,512]{2,1,0:T(8,128)(2,1)S(1)}, bf16[1,256,512]{2,1,0:T(8,128)(2,1)}, u32[]{:S(2)}) copy-start(bf16[1,256,512]{2,1,0:T(8,128)(2,1)} %copy-done.2) | copy-start | bytes 786436
Sparse Core Ops, SparseCore 0:
  11.1 29.8 all-gather.4
  42.6 27.4 all-gather.8
  71.9 27.9 all-gather.6
  101.7 27.8 all-gather.10
